TPU v7x, 32 devices: a whole 2x2x4 slice. The times are simulated.
32 devices in a mesh: cuts: 4 (over x, core), dom: 4 (over z), vec: 2 (over y).
Axes of the slice: x: 2, y: 2, z: 4, core: 2. Of those that a mesh axis runs over, the one named last changes fastest.
Arguments:
- starts_old: bfloat16 [4, 2, 32, 384, 768], P('cuts', None, 'vec', 'dom'), may hold values from -6 to 6
- y_operator: bfloat16 [768, 768], replicated, may hold values from -0.21875 to 0.21875
- coarse_inverse: bfloat16 [384, 384], P('vec'), may hold values from -1 to 2
- base_speed: float32 [384, 768], P('dom'), may hold values from 0.5 to 1.5
- damping: float32 [32], P('vec'), may hold values from 0.5 to 3
- coupling: float32 [32], P('vec'), may hold values from 0.3 to 1.5
Outputs:
- ends_new: float32 [4, 2, 32, 384, 768], P('cuts', None, 'vec', 'dom')
All inputs are finite; a program needn't handle non-finite values.
Results may differ from a plain program's by a relative error of at most 0.0078.
Values may be sent and summed in bfloat16 or wider, within the bound.
No kernel may reach another device: no remote copies, remote signals or barrier semaphores. Data moves between devices by JAX's collectives and lax.ppermute only.
A program may use at most 192 MiB of HBM per device.

v0:
```python
import jax
import jax.numpy as jnp
import numpy as np
from jax import lax
from jax.sharding import PartitionSpec as P

NP = 16
fine_step = 0.25
penalty = 2.0


def from_behind(shard, axis, by):
    size = lax.axis_size(axis)
    pairs = [(i, i + by) for i in range(size) if 0 <= i + by < size]
    return lax.ppermute(shard, axis, pairs)


def cheb_matrix(points_sub):
    indices = np.arange(points_sub)
    points = -np.cos(np.pi * indices / (points_sub - 1))
    edge_weight = np.where((indices == 0) | (indices == points_sub - 1), 2.0, 1.0)
    sign_table = np.where((indices[:, None] + indices[None, :]) % 2 == 0, 1.0, -1.0)
    identity_table = np.eye(points_sub)
    gap_matrix = points[:, None] - points[None, :] + identity_table
    off_diag = (
        edge_weight[:, None]
        / edge_weight[None, :]
        * sign_table
        / gap_matrix
        * (1.0 - identity_table)
    )
    return off_diag - off_diag.sum(axis=1)[:, None] * identity_table


def local(starts_old, y_operator, coarse_inverse, base_speed, damping, coupling):
    start_block = starts_old[0]
    current_state = start_block.astype(jnp.float32)
    part_count, wave_count, column_count, y_count = current_state.shape
    points_sub = NP
    sub_count = column_count // points_sub
    x_scale = 4.0 / (points_sub * points_sub)
    derivative = jnp.asarray(cheb_matrix(points_sub), jnp.float32)
    sign_factor = jnp.array([1.0, -1.0], jnp.float32)[:, None, None, None]
    first_point = (jnp.arange(column_count) % points_sub == 0).astype(jnp.float32)[
        None, None, :, None
    ]
    speed_field = base_speed[None, None]
    full_inverse = lax.all_gather(coarse_inverse, "vec", axis=0, tiled=True)

    def slope_of(values):
        rounded = values.astype(jnp.bfloat16)
        along_y = jnp.dot(
            rounded.reshape(part_count * wave_count * column_count, y_count),
            y_operator,
            preferred_element_type=jnp.float32,
        ).reshape(values.shape)
        blocks = values.reshape(part_count, wave_count, sub_count, points_sub, y_count)
        along_x = jnp.einsum(
            "ij,pwsjy->pwsiy", derivative, blocks, precision=lax.Precision.HIGHEST
        ).reshape(values.shape)
        inflow_row = from_behind(values[:, :, column_count - 1 :, :], "dom", 1)
        previous = jnp.concatenate([inflow_row, values[:, :, : column_count - 1, :]], axis=2)
        jump_term = first_point * (values - previous)
        advect = speed_field * (x_scale * along_x + penalty * jump_term)
        partner = rounded[::-1].astype(jnp.float32)
        return (
            -advect
            + along_y
            + sign_factor * coupling[None, :, None, None] * partner
            - damping[None, :, None, None] * values
        )

    middle = current_state + fine_step * slope_of(current_state)
    fine_end = middle + fine_step * slope_of(middle)
    factor = 1.0 / (1.0 + 2.0 * fine_step * damping)
    is_leader = lax.axis_index("cuts") == 0
    slice_total = lax.axis_size("cuts")
    line_waves = wave_count // lax.axis_size("dom")
    gain = lax.dynamic_slice_in_dim(factor, lax.axis_index("dom") * line_waves, line_waves, 0)[
        None, :, None, None
    ]
    fine_lines = lax.all_to_all(fine_end, "dom", split_axis=1, concat_axis=2, tiled=True)
    start_lines = lax.all_to_all(start_block, "dom", split_axis=1, concat_axis=2, tiled=True)
    line_state = fine_lines
    start_wide = start_lines.astype(jnp.float32)
    for turn_index in range(slice_total - 1):
        arrived = from_behind(line_state.astype(jnp.bfloat16), "cuts", 1)
        gap = (arrived.astype(jnp.float32) - start_wide).astype(jnp.bfloat16)
        mapped = jnp.einsum("ij,pwjy->pwiy", full_inverse, gap, preferred_element_type=jnp.float32)
        line_state = jnp.where(is_leader, fine_lines, fine_lines + gain * mapped)
    block_state = lax.all_to_all(line_state, "dom", split_axis=2, concat_axis=1, tiled=True)
    return block_state[None]


def solution(mesh):
    in_specs = (
        P("cuts", None, "vec", "dom", None),
        P(),
        P("vec", None),
        P("dom", None),
        P("vec"),
        P("vec"),
    )
    out_specs = P("cuts", None, "vec", "dom", None)
    return jax.shard_map(local, mesh=mesh, in_specs=in_specs, out_specs=out_specs, check_vma=False)
```

profile of v0, /device:TPU:1, one launch (start us, length us, event | category | flops | bytes accessed | tf_op | source)
XLA Modules:
  0.0 757.5 jit_solution(18012509088474431244)
XLA Ops:
  0.0 3.6 bitcast_convert_fusion.1
  3.7 3.7 copy-done.5
  7.5 4.0 collective-permute-start
  11.7 6.4 broadcast_multiply_fusion
  18.1 17.1 %fusion.30 = (bf16[2,16,96,768]{3,2,1,0:T(8,128)(2,1)}, f32[2,16,96,768]{3,2,1,0:T(8,128)}) fusion(f32[16]{0:T(128)S(1)} %copy-done.11, bf16[2,16,96,768]{3,2,1,0:T(8,128)(2,1)S(1)} %bitcast.66, f32[2,16]{1,0:T(2,128)S(1)} %broadcast_multiply_fusion.2, bf16[768,768]{1,0:T(8,128)(2,1)S(1)} %copy-done, f32[2,16,95,768]{3,2,1,0:T(8,128)} %bitcast.71, ...), kind=kOutput, calls=%fused_computation.47 | convolution fusion | flops 3663986688 | bytes 39223872 | tf_op jit(solution)/shard_map/dot_general | solution.py:52
  36.3 3.4 collective-permute-start.1
  39.7 12.9 %broadcast_multiply_fusion.1 = f32[2,16,6,768,16]{3,4,2,1,0:T(8,128)} fusion(f32[2,16,6,16,768]{4,3,2,1,0:T(8,128)} %bitcast.69, f32[16,16,1,1,1]{1,0,4,3,2:T(8,128)S(1)} %copy-done.7), kind=kOutput, calls=%fused_computation.35 | convolution fusion | flops 455344128 | bytes 18875392 | tf_op jit(solution)/shard_map/ij,pwsjy->pwsiy/dot_general | solution.py:58
  52.6 19.1 %fusion.21 = f32[2,16,96,768]{3,2,1,0:T(8,128)} fusion(f32[2,16,96,768]{3,2,1,0:T(8,128)} %get-tuple-element.6, f32[2,16,95,768]{3,2,1,0:T(8,128)} %bitcast.70, f32[2,16,1,768]{3,2,1,0:T(1,128)S(1)} %collective-permute-done.1, f32[2,16,6,768,16]{3,4,2,1,0:T(8,128)} %broadcast_multiply_fusion.1, bf16[2,16,96,768]{3,2,1,0:T(8,128)(2,1)} %get-tuple-element.5, ...), kind=kOutput, calls=%fused_computation.26 | convolution fusion | flops 3659268096 | bytes 43942464 | tf_op jit(solution)/shard_map/dot_general | solution.py:52
  71.7 8.4 %copy.50 = f32[2,16,96,768]{3,2,0,1:T(8,128)} copy(f32[2,16,96,768]{3,2,1,0:T(8,128)} %fusion.21) | data formatting | bytes 18874368 | tf_op jit(solution)/shard_map/add | solution.py:74
  80.1 5.8 all-to-all-start
  86.0 4.9 copy.53
  90.8 200.3 %all-to-all-done = f32[2,16,96,768]{3,2,0,1:T(8,128)} async-done(((f32[2,16,96,768]{3,2,0,1:T(8,128)}), f32[2,16,96,768]{3,2,0,1:T(8,128)}, u32[]{:S(2)}, u32[]{:S(2)}) %all-to-all-start) | async-done | bytes 9437216 | tf_op jit(solution)/shard_map/all_to_all | solution.py:82
  291.1 5.0 all-to-all-start.1
  296.1 4.7 copy.52
  300.8 3.7 copy-done.2
  307.2 4.4 collective-permute-start.2
  311.7 5.9 all_gather.3
  317.6 82.4 %all-to-all-done.1 = bf16[2,16,96,768]{3,2,0,1:T(8,128)(2,1)} async-done(((bf16[2,16,96,768]{3,2,0,1:T(8,128)(2,1)}), bf16[2,16,96,768]{3,2,0,1:T(8,128)(2,1)}, u32[]{:S(2)}, u32[]{:S(2)}) %all-to-all-start.1) | async-done | bytes 4718624 | tf_op jit(solution)/shard_map/all_to_all | solution.py:83
  403.9 4.7 copy.55
  408.6 9.6 %copy.64 = f32[2,4,384,768]{2,3,1,0:T(8,128)} copy(f32[2,4,384,768]{3,2,1,0:T(8,128)} %bitcast.61) | data formatting | bytes 18874368 | tf_op jit(solution)/shard_map/all_to_all | solution.py:82
  418.2 13.9 %fusion = bf16[2,4,384,768]{2,3,1,0:T(8,128)(2,1)} fusion(f32[2,4,384,768]{2,3,1,0:T(8,128)} %copy.64, f32[4]{0:T(128)S(1)} %dynamic_slice.3, pred[]{:T(512)S(6)} %eq.15, f32[2,4,384,768]{3,2,1,0:T(8,128)} %bitcast.62, bf16[2,4,384,768]{3,2,1,0:T(8,128)(2,1)} %collective-permute-done.2, bf16[384,384]{1,0:T(8,128)(2,1)S(1)} %all_gather.3), kind=kOutput, calls=%fused_computation.3 | convolution fusion | flops 1828454400 | bytes 28606480 | tf_op jit(solution)/shard_map/ij,pwjy->pwiy/dot_general | solution.py:89
  432.1 4.4 collective-permute-start.3
  436.5 9.6 %copy.59 = f32[2,4,384,768]{2,3,1,0:T(8,128)} copy(f32[2,4,384,768]{3,2,1,0:T(8,128)} %bitcast.63) | data formatting | bytes 18874368 | tf_op jit(solution)/shard_map/convert_element_type | solution.py:85
  446.1 41.8 %collective-permute-done.3 = bf16[2,4,384,768]{2,3,1,0:T(8,128)(2,1)} collective-permute-done((bf16[2,4,384,768]{2,3,1,0:T(8,128)(2,1)}, bf16[2,4,384,768]{2,3,1,0:T(8,128)(2,1)}, u32[]{:S(2)}, u32[]{:S(2)}) %collective-permute-start.3) | collective-permute-done | bytes 4718624 | tf_op jit(solution)/shard_map/ppermute | solution.py:15
  487.9 13.5 %fusion.1 = bf16[2,4,384,768]{2,3,1,0:T(8,128)(2,1)} fusion(f32[2,4,384,768]{2,3,1,0:T(8,128)} %copy.64, f32[4]{0:T(128)S(1)} %dynamic_slice.3, pred[]{:T(512)S(6)} %eq.15, f32[2,4,384,768]{2,3,1,0:T(8,128)} %copy.59, bf16[2,4,384,768]{2,3,1,0:T(8,128)(2,1)} %collective-permute-done.3, bf16[384,384]{1,0:T(8,128)(2,1)S(1)} %all_gather.3), kind=kOutput, calls=%fused_computation.4 | convolution fusion | flops 1828454400 | bytes 28606480 | tf_op jit(solution)/shard_map/ij,pwjy->pwiy/dot_general | solution.py:89
  501.4 4.6 collective-permute-start.4
  506.0 51.1 %collective-permute-done.4 = bf16[2,4,384,768]{2,3,1,0:T(8,128)(2,1)S(1)} collective-permute-done((bf16[2,4,384,768]{2,3,1,0:T(8,128)(2,1)}, bf16[2,4,384,768]{2,3,1,0:T(8,128)(2,1)S(1)}, u32[]{:S(2)}, u32[]{:S(2)}) %collective-permute-start.4) | collective-permute-done | bytes 4718624 | tf_op jit(solution)/shard_map/ppermute | solution.py:15
  557.1 8.0 %add_select_fusion = f32[2,4,384,768]{2,3,1,0:T(8,128)} fusion(f32[2,4,384,768]{2,3,1,0:T(8,128)} %copy.64, f32[4]{0:T(128)S(1)} %dynamic_slice.3, pred[]{:T(512)S(6)} %eq.15, f32[2,4,384,768]{2,3,1,0:T(8,128)S(1)} %copy-done.3, bf16[2,4,384,768]{2,3,1,0:T(8,128)(2,1)S(1)} %collective-permute-done.4, bf16[384,384]{1,0:T(8,128)(2,1)S(1)} %all_gather.3), kind=kOutput, calls=%fused_computation | convolution fusion | flops 1826095104 | bytes 33325072 | tf_op jit(solution)/shard_map/ij,pwjy->pwiy/dot_general | solution.py:89
  565.2 12.5 %copy.65 = f32[2,4,384,768]{3,1,0,2:T(4,128)} copy(f32[2,4,384,768]{2,3,1,0:T(8,128)} %add_select_fusion) | data formatting | bytes 18874368 | tf_op jit(solution)/shard_map/jit(_where)/select_n | solution.py:90
  577.6 164.8 %all_to_all.42 = f32[2,4,384,768]{3,1,0,2:T(4,128)S(1)} all-to-all(f32[2,4,384,768]{3,1,0,2:T(4,128)} %copy.65), channel_id=1, replica_groups=mesh['cuts'=4,'dom'=4,'vec'=2] {'dom'}, dimensions={2} | all-to-all | bytes 18874368 | tf_op jit(solution)/shard_map/all_to_all | solution.py:91
  742.5 6.6 copy.66
  749.0 8.5 %copy.67 = f32[2,4,4,96,768]{4,3,2,1,0:T(8,128)} copy(f32[2,4,4,96,768]{4,3,1,2,0:T(8,128)} %bitcast.67) | data formatting | bytes 18874368 | tf_op jit(solution)/shard_map/all_to_all | solution.py:91
  (34 shorter events, 8.0 us)
Async XLA Ops:
  0.0 18.0 %copy-start = (bf16[768,768]{1,0:T(8,128)(2,1)S(1)}, bf16[768,768]{1,0:T(8,128)(2,1)}, u32[]{:S(2)}) copy-start(bf16[768,768]{1,0:T(8,128)(2,1)} %param.9) | copy-start | bytes 3538948
  0.0 11.6 %copy-start.9 = (f32[2]{0:T(128)S(1)}, f32[2]{0:T(128)}, u32[]{:S(2)}) copy-start(f32[2]{0:T(128)} %constant.44.clone) | copy-start | bytes 28
  0.0 11.7 %copy-start.7 = (f32[16,16,1,1,1]{1,0,4,3,2:T(8,128)S(1)}, f32[16,16,1,1,1]{1,0,4,3,2:T(8,128)}, u32[]{:S(2)}) copy-start(f32[16,16,1,1,1]{1,0,4,3,2:T(8,128)} %constant.46) | copy-start | bytes 3076
  0.0 11.6 %copy-start.4 = (bf16[1,2,16,96,768]{4,3,2,1,0:T(8,128)(2,1)S(1)}, bf16[1,2,16,96,768]{4,3,2,1,0:T(8,128)(2,1)}, u32[]{:S(2)}) copy-start(bf16[1,2,16,96,768]{4,3,2,1,0:T(8,128)(2,1)} %param.8) | copy-start | bytes 14155780
  0.0 11.5 %copy-start.8 = (f32[16]{0:T(128)S(1)}, f32[16]{0:T(128)}, u32[]{:S(2)}) copy-start(f32[16]{0:T(128)} %param.13) | copy-start | bytes 196
  3.7 3.7 copy-start.5
  7.4 10.6 %copy-start.10 = (f32[96,768]{1,0:T(8,128)S(1)}, f32[96,768]{1,0:T(8,128)}, u32[]{:S(2)}) copy-start(f32[96,768]{1,0:T(8,128)} %param.11) | copy-start | bytes 884740
  7.4 10.6 %copy-start.11 = (f32[16]{0:T(128)S(1)}, f32[16]{0:T(128)}, u32[]{:S(2)}) copy-start(f32[16]{0:T(128)} %param.12) | copy-start | bytes 196
  7.5 10.5 %collective-permute-start = (f32[2,16,1,768]{3,2,1,0:T(1,128)S(1)}, f32[2,16,1,768]{3,2,1,0:T(1,128)S(1)}, u32[]{:S(2)}, u32[]{:S(2)}) collective-permute-start(f32[2,16,1,768]{3,2,1,0:T(1,128)S(1)} %slice.16), channel_id=1, source_target_pairs={{0,2},{2,4},{4,6},{1,3},{3,5},{5,7},{8,10},{10,12},{12,14},{9,11},... | collective-permute-start | bytes 294920 | tf_op jit(solution)/shard_map/ppermute | solution.py:15
  36.3 16.3 %collective-permute-start.1 = (f32[2,16,1,768]{3,2,1,0:T(1,128)S(1)}, f32[2,16,1,768]{3,2,1,0:T(1,128)S(1)}, u32[]{:S(2)}, u32[]{:S(2)}) collective-permute-start(f32[2,16,1,768]{3,2,1,0:T(1,128)S(1)} %slice.18), channel_id=1, source_target_pairs={{0,2},{2,4},{4,6},{1,3},{3,5},{5,7},{8,10},{10,12},{12,14},{9,11},... | collective-permute-start | bytes 294920 | tf_op jit(solution)/shard_map/ppermute | solution.py:15
  80.1 210.9 %all-to-all-start = ((f32[2,16,96,768]{3,2,0,1:T(8,128)}), f32[2,16,96,768]{3,2,0,1:T(8,128)}, u32[]{:S(2)}, u32[]{:S(2)}) async-start(f32[2,16,96,768]{3,2,0,1:T(8,128)} %copy.50), calls=%async_computation | async-start | bytes 18874368 | tf_op jit(solution)/shard_map/all_to_all | solution.py:82
  291.1 109.0 %all-to-all-start.1 = ((bf16[2,16,96,768]{3,2,0,1:T(8,128)(2,1)}), bf16[2,16,96,768]{3,2,0,1:T(8,128)(2,1)}, u32[]{:S(2)}, u32[]{:S(2)}) async-start(bf16[2,16,96,768]{3,2,0,1:T(8,128)(2,1)} %copy.53), calls=%async_computation.1 | async-start | bytes 9437184 | tf_op jit(solution)/shard_map/all_to_all | solution.py:83
  300.8 3.7 copy-start.2
  304.5 7.2 copy-start.6
  307.2 111.0 %collective-permute-start.2 = (bf16[2,4,384,768]{3,2,1,0:T(8,128)(2,1)}, bf16[2,4,384,768]{3,2,1,0:T(8,128)(2,1)}, u32[]{:S(2)}, u32[]{:S(2)}) collective-permute-start(bf16[2,4,384,768]{3,2,1,0:T(8,128)(2,1)} %bitcast_convert_fusion), channel_id=1, source_target_pairs={{0,8},{8,16},{16,24},{1,9},{9,17},{17,25},{2,10},{10,18},{18,26},{... | collective-permute-start | bytes 14155784 | tf_op jit(solution)/shard_map/ppermute | solution.py:15
  432.1 55.8 %collective-permute-start.3 = (bf16[2,4,384,768]{2,3,1,0:T(8,128)(2,1)}, bf16[2,4,384,768]{2,3,1,0:T(8,128)(2,1)}, u32[]{:S(2)}, u32[]{:S(2)}) collective-permute-start(bf16[2,4,384,768]{2,3,1,0:T(8,128)(2,1)} %fusion), channel_id=1, source_target_pairs={{0,8},{8,16},{16,24},{1,9},{9,17},{17,25},{2,10},{10,18},{18,26},{... | collective-permute-start | bytes 14155784 | tf_op jit(solution)/shard_map/ppermute | solution.py:15
  446.1 111.0 %copy-start.3 = (f32[2,4,384,768]{2,3,1,0:T(8,128)S(1)}, f32[2,4,384,768]{2,3,1,0:T(8,128)}, u32[]{:S(2)}) copy-start(f32[2,4,384,768]{2,3,1,0:T(8,128)} %copy.59) | copy-start | bytes 28311556
  501.4 55.7 %collective-permute-start.4 = (bf16[2,4,384,768]{2,3,1,0:T(8,128)(2,1)}, bf16[2,4,384,768]{2,3,1,0:T(8,128)(2,1)S(1)}, u32[]{:S(2)}, u32[]{:S(2)}) collective-permute-start(bf16[2,4,384,768]{2,3,1,0:T(8,128)(2,1)} %fusion.1), channel_id=1, source_target_pairs={{0,8},{8,16},{16,24},{1,9},{9,17},{17,25},{2,10},{10,18},{18,26},{... | collective-permute-start | bytes 14155784 | tf_op jit(solution)/shard_map/ppermute | solution.py:15
  749.0 8.5 %copy-start.1 = (bf16[768,768]{1,0:T(8,128)(2,1)S(1)}, bf16[768,768]{1,0:T(8,128)(2,1)}, u32[]{:S(2)}) copy-start(bf16[768,768]{1,0:T(8,128)(2,1)} %param.9) | copy-start | bytes 3538948
where the time goes:
time: 759 us; the launch traced here: 758 us
  waiting for transfers between devices  376 us (50%)
  blocking collectives  171 us (23%)
  matrix products  90.9 us (12%)
  local copies, waits for them, and re-layouts  81 us (11%)
  starting transfers between devices  31.6 us (4%)
    all_to_all x1, waiting for transfers between devices, local(): lax.all_to_all(fine_end, 'dom', split_axis=1, concat_axis=2, tiled=True)  200 us
    all_to_all x1, blocking collectives, local(): lax.all_to_all(line_state, 'dom', split_axis=2, concat_axis=1, tiled=True)  165 us
    ppermute x5, waiting for transfers between devices, from_behind(): return lax.ppermute(shard, axis, pairs)  92.9 us
    all_to_all x1, waiting for transfers between devices, local(): lax.all_to_all(start_block, 'dom', split_axis=1, concat_axis=2, tiled=True)  82.4 us
    dot_general x2, matrix products, slope_of(): jnp.dot(rounded.reshape(part_count * wave_count * column_count, y_count),...  36.1 us
    dot_general x3, matrix products, local(): jnp.einsum('ij,pwjy->pwiy', full_inverse, gap, preferred_element_type=jnp...  35.5 us
    ppermute x5, starting transfers between devices, from_behind(): return lax.ppermute(shard, axis, pairs)  20.8 us
    dot_general x2, matrix products, slope_of(): jnp.einsum('ij,pwsjy->pwsiy', derivative, blocks, precision=lax.Precision...  19.3 us
  transfers between devices with their start and end apart: 7, of which 4 were waited for; matrix products, arithmetic and copies ran while one was open for 8% of the time, Pallas kernels for 0%

commit v1 on v0

--- a/solution.py
+++ b/solution.py
@@ -88,7 +88,23 @@
         gap = (arrived.astype(jnp.float32) - start_wide).astype(jnp.bfloat16)
         mapped = jnp.einsum("ij,pwjy->pwiy", full_inverse, gap, preferred_element_type=jnp.float32)
         line_state = jnp.where(is_leader, fine_lines, fine_lines + gain * mapped)
-    block_state = lax.all_to_all(line_state, "dom", split_axis=2, concat_axis=1, tiled=True)
+
+    def replace_sheet_on(raw, axis_id):
+        side_arr, state_now = (lax.axis_size(axis_id), lax.axis_index(axis_id))
+        u_next = raw.shape[2] // side_arr
+        part_next = list(raw.shape)
+        part_next[2] = u_next
+        x_next = part_next[1]
+        part_next[1] = x_next * side_arr
+        a_now = jnp.zeros(part_next, raw.dtype)
+        for u in range(side_arr):
+            big = lax.dynamic_slice_in_dim(raw, (state_now ^ u) * u_next, u_next, axis=2)
+            if u:
+                big = lax.ppermute(big, axis_id, [(h, h ^ u) for h in range(side_arr)])
+            a_now = lax.dynamic_update_slice_in_dim(a_now, big, (state_now ^ u) * x_next, axis=1)
+        return a_now
+
+    block_state = replace_sheet_on(line_state, "dom")
     return block_state[None]
 
 

time: 759 us -> 728 us (0.959)
  the two profiles are of different devices: /device:TPU:1 before, /device:TPU:10 now
where the time goes in v1:
time: 728 us
  waiting for transfers between devices  537 us (74%)
  matrix products  71.6 us (10%)
  local copies, waits for them, and re-layouts  49.4 us (7%)
  starting transfers between devices  32.2 us (4%)
  other arithmetic  31.4 us (4%)
    all_to_all x1, waiting for transfers between devices, local(): lax.all_to_all(fine_end, 'dom', split_axis=1, concat_axis=2, tiled=True)  197 us
    ppermute x3, waiting for transfers between devices, replace_sheet_on(): big = lax.ppermute(big, axis_id, [(h, h ^ u) for h in range(side_arr)])  151 us
    ppermute x5, waiting for transfers between devices, from_behind(): return lax.ppermute(shard, axis, pairs)  107 us
    all_to_all x1, waiting for transfers between devices, local(): lax.all_to_all(start_block, 'dom', split_axis=1, concat_axis=2, tiled=True)  81.5 us
    dot_general x2, matrix products, slope_of(): jnp.dot(rounded.reshape(part_count * wave_count * column_count, y_count),...  35.5 us
    convert_element_type x3, other arithmetic, local(): gap = (arrived.astype(jnp.float32) - start_wide).astype(jnp.bfloat16)  25 us
    dot_general x2, matrix products, slope_of(): jnp.einsum('ij,pwsjy->pwsiy', derivative, blocks, precision=lax.Precision...  19.4 us
    dot_general x3, matrix products, local(): jnp.einsum('ij,pwjy->pwiy', full_inverse, gap, preferred_element_type=jnp...  16.7 us
  transfers between devices with their start and end apart: 10, of which 7 were waited for; matrix products, arithmetic and copies ran while one was open for 6% of the time, Pallas kernels for 0%

profile of v1, /device:TPU:10, one launch (start us, length us, event | category | flops | bytes accessed | tf_op | source)
XLA Modules:
  0.0 727.5 jit_solution(13482491418694279199)
XLA Ops:
  0.0 3.6 bitcast_convert_fusion.1
  3.7 3.7 copy-done.5
  7.5 3.5 collective-permute-start
  11.1 6.4 broadcast_multiply_fusion
  17.6 16.7 %fusion.30 = (bf16[2,16,96,768]{3,2,1,0:T(8,128)(2,1)}, f32[2,16,96,768]{3,2,1,0:T(8,128)}) fusion(f32[16]{0:T(128)S(1)} %copy-done.12, bf16[2,16,96,768]{3,2,1,0:T(8,128)(2,1)S(1)} %bitcast.86, f32[2,16]{1,0:T(2,128)S(1)} %broadcast_multiply_fusion.2, bf16[768,768]{1,0:T(8,128)(2,1)S(1)} %copy-done, f32[2,16,95,768]{3,2,1,0:T(8,128)} %bitcast.89, ...), kind=kOutput, calls=%fused_computation.53 | convolution fusion | flops 3663986688 | bytes 39223872 | tf_op jit(solution)/shard_map/dot_general | solution.py:52
  35.5 3.7 collective-permute-start.1
  39.2 12.9 %broadcast_multiply_fusion.1 = f32[2,16,6,768,16]{3,4,2,1,0:T(8,128)} fusion(f32[2,16,6,16,768]{4,3,2,1,0:T(8,128)} %bitcast.87, f32[16,16,1,1,1]{1,0,4,3,2:T(8,128)S(1)} %copy-done.8), kind=kOutput, calls=%fused_computation.35 | convolution fusion | flops 455344128 | bytes 18875392 | tf_op jit(solution)/shard_map/ij,pwsjy->pwsiy/dot_general | solution.py:58
  52.1 18.8 %fusion.21 = f32[2,16,96,768]{3,2,1,0:T(8,128)} fusion(f32[2,16,96,768]{3,2,1,0:T(8,128)} %get-tuple-element.9, f32[2,16,95,768]{3,2,1,0:T(8,128)} %bitcast.88, f32[2,16,1,768]{3,2,1,0:T(1,128)S(1)} %collective-permute-done.1, f32[2,16,6,768,16]{3,4,2,1,0:T(8,128)} %broadcast_multiply_fusion.1, bf16[2,16,96,768]{3,2,1,0:T(8,128)(2,1)} %get-tuple-element.8, ...), kind=kOutput, calls=%fused_computation.26 | convolution fusion | flops 3659268096 | bytes 43942464 | tf_op jit(solution)/shard_map/dot_general | solution.py:52
  70.9 8.4 %copy.11 = f32[2,16,96,768]{3,2,0,1:T(8,128)} copy(f32[2,16,96,768]{3,2,1,0:T(8,128)} %fusion.21) | data formatting | bytes 18874368 | tf_op jit(solution)/shard_map/add | solution.py:74
  79.3 6.2 all-to-all-start
  85.5 4.9 copy.13
  90.4 197.1 %all-to-all-done = f32[2,16,96,768]{3,2,0,1:T(8,128)} async-done(((f32[2,16,96,768]{3,2,0,1:T(8,128)}), f32[2,16,96,768]{3,2,0,1:T(8,128)}, u32[]{:S(2)}, u32[]{:S(2)}) %all-to-all-start) | async-done | bytes 9437216 | tf_op jit(solution)/shard_map/all_to_all | solution.py:82
  287.4 8.3 %all-to-all-start.1 = ((bf16[2,16,96,768]{3,2,0,1:T(8,128)(2,1)}), bf16[2,16,96,768]{3,2,0,1:T(8,128)(2,1)}, u32[]{:S(2)}, u32[]{:S(2)}) async-start(bf16[2,16,96,768]{3,2,0,1:T(8,128)(2,1)} %copy.13), calls=%async_computation.1 | async-start | bytes 9437184 | tf_op jit(solution)/shard_map/all_to_all | solution.py:83
  295.7 4.7 copy.12
  300.4 3.7 copy-done.2
  308.8 6.0 all_gather.3
  314.8 81.5 %all-to-all-done.1 = bf16[2,16,96,768]{3,2,0,1:T(8,128)(2,1)} async-done(((bf16[2,16,96,768]{3,2,0,1:T(8,128)(2,1)}), bf16[2,16,96,768]{3,2,0,1:T(8,128)(2,1)}, u32[]{:S(2)}, u32[]{:S(2)}) %all-to-all-start.1) | async-done | bytes 4718624 | tf_op jit(solution)/shard_map/all_to_all | solution.py:83
  396.4 7.3 %copy.14 = f32[2,4,4,96,768]{4,3,1,2,0:T(8,128)} copy(bf16[2,4,4,96,768]{4,3,0,2,1:T(8,128)(2,1)} %bitcast.31) | data formatting | bytes 14155776 | tf_op jit(solution)/shard_map/convert_element_type | solution.py:85
  403.7 8.4 %fusion.22 = bf16[2,4,384,768]{3,2,1,0:T(8,128)(2,1)} fusion(f32[2,4,4,96,768]{4,3,1,2,0:T(8,128)} %copy.14, bf16[2,4,384,768]{3,2,1,0:T(8,128)(2,1)} %collective-permute-done.2), kind=kLoop, calls=%fused_computation.30 | loop fusion | flops 7077888 | bytes 18874368 | tf_op jit(solution)/shard_map/convert_element_type | solution.py:88
  412.1 5.3 fusion
  419.4 53.6 %collective-permute-done.3 = bf16[2,4,384,768]{3,2,1,0:T(8,128)(2,1)} collective-permute-done((bf16[2,4,384,768]{3,2,1,0:T(8,128)(2,1)S(1)}, bf16[2,4,384,768]{3,2,1,0:T(8,128)(2,1)}, u32[]{:S(2)}, u32[]{:S(2)}) %collective-permute-start.3) | collective-permute-done | bytes 4718624 | tf_op jit(solution)/shard_map/ppermute | solution.py:15
  473.0 8.3 %fusion.23 = bf16[2,4,384,768]{3,2,1,0:T(8,128)(2,1)} fusion(f32[2,4,4,96,768]{4,3,1,2,0:T(8,128)} %copy.14, bf16[2,4,384,768]{3,2,1,0:T(8,128)(2,1)} %collective-permute-done.3), kind=kLoop, calls=%fused_computation.31 | loop fusion | flops 7077888 | bytes 18874368 | tf_op jit(solution)/shard_map/convert_element_type | solution.py:88
  481.4 6.7 fusion.1
  490.0 53.8 %collective-permute-done.4 = bf16[2,4,384,768]{3,2,1,0:T(8,128)(2,1)} collective-permute-done((bf16[2,4,384,768]{3,2,1,0:T(8,128)(2,1)}, bf16[2,4,384,768]{3,2,1,0:T(8,128)(2,1)}, u32[]{:S(2)}, u32[]{:S(2)}) %collective-permute-start.4) | collective-permute-done | bytes 4718624 | tf_op jit(solution)/shard_map/ppermute | solution.py:15
  543.8 8.3 %fusion.24 = bf16[2,4,384,768]{3,2,1,0:T(8,128)(2,1)} fusion(f32[2,4,4,96,768]{4,3,1,2,0:T(8,128)} %copy.14, bf16[2,4,384,768]{3,2,1,0:T(8,128)(2,1)} %collective-permute-done.4), kind=kLoop, calls=%fused_computation.32 | loop fusion | flops 7077888 | bytes 18874368 | tf_op jit(solution)/shard_map/convert_element_type | solution.py:88
  552.1 4.7 add_select_fusion
  556.8 3.7 copy-done.4
  560.5 3.0 constant_dynamic-slice_fusion
  563.5 3.4 collective-permute-start.5
  571.4 63.8 %collective-permute-done.5 = f32[2,4,96,768]{3,2,1,0:T(8,128)} collective-permute-done((f32[2,4,96,768]{3,2,1,0:T(8,128)}, f32[2,4,96,768]{3,2,1,0:T(8,128)}, u32[]{:S(2)}, u32[]{:S(2)}) %collective-permute-start.5) | collective-permute-done | bytes 2359328 | tf_op jit(solution)/shard_map/ppermute | solution.py:103
  637.0 61.7 %collective-permute-done.6 = f32[2,4,96,768]{3,2,1,0:T(8,128)} collective-permute-done((f32[2,4,96,768]{3,2,1,0:T(8,128)}, f32[2,4,96,768]{3,2,1,0:T(8,128)}, u32[]{:S(2)}, u32[]{:S(2)}) %collective-permute-start.6) | collective-permute-done | bytes 2359328 | tf_op jit(solution)/shard_map/ppermute | solution.py:103
  700.7 25.2 %collective-permute-done.7 = f32[2,4,96,768]{3,2,1,0:T(8,128)S(1)} collective-permute-done((f32[2,4,96,768]{3,2,1,0:T(8,128)}, f32[2,4,96,768]{3,2,1,0:T(8,128)S(1)}, u32[]{:S(2)}, u32[]{:S(2)}) %collective-permute-start.7) | collective-permute-done | bytes 2359328 | tf_op jit(solution)/shard_map/ppermute | solution.py:103
  (57 shorter events, 19.8 us)
Async XLA Ops:
  0.0 17.6 %copy-start = (bf16[768,768]{1,0:T(8,128)(2,1)S(1)}, bf16[768,768]{1,0:T(8,128)(2,1)}, u32[]{:S(2)}) copy-start(bf16[768,768]{1,0:T(8,128)(2,1)} %param.9) | copy-start | bytes 3538948
  0.0 11.0 %copy-start.10 = (f32[2]{0:T(128)S(1)}, f32[2]{0:T(128)}, u32[]{:S(2)}) copy-start(f32[2]{0:T(128)} %constant.60.clone) | copy-start | bytes 28
  0.0 11.1 %copy-start.8 = (f32[16,16,1,1,1]{1,0,4,3,2:T(8,128)S(1)}, f32[16,16,1,1,1]{1,0,4,3,2:T(8,128)}, u32[]{:S(2)}) copy-start(f32[16,16,1,1,1]{1,0,4,3,2:T(8,128)} %constant.62) | copy-start | bytes 3076
  0.0 11.1 %copy-start.3 = (bf16[1,2,16,96,768]{4,3,2,1,0:T(8,128)(2,1)S(1)}, bf16[1,2,16,96,768]{4,3,2,1,0:T(8,128)(2,1)}, u32[]{:S(2)}) copy-start(bf16[1,2,16,96,768]{4,3,2,1,0:T(8,128)(2,1)} %param.8) | copy-start | bytes 14155780
  0.0 11.0 %copy-start.9 = (f32[16]{0:T(128)S(1)}, f32[16]{0:T(128)}, u32[]{:S(2)}) copy-start(f32[16]{0:T(128)} %param.13) | copy-start | bytes 196
  3.7 3.7 copy-start.5
  7.4 10.1 %copy-start.11 = (f32[96,768]{1,0:T(8,128)S(1)}, f32[96,768]{1,0:T(8,128)}, u32[]{:S(2)}) copy-start(f32[96,768]{1,0:T(8,128)} %param.11) | copy-start | bytes 884740
  7.4 10.1 %copy-start.12 = (f32[16]{0:T(128)S(1)}, f32[16]{0:T(128)}, u32[]{:S(2)}) copy-start(f32[16]{0:T(128)} %param.12) | copy-start | bytes 196
  7.5 10.0 %collective-permute-start = (f32[2,16,1,768]{3,2,1,0:T(1,128)S(1)}, f32[2,16,1,768]{3,2,1,0:T(1,128)S(1)}, u32[]{:S(2)}, u32[]{:S(2)}) collective-permute-start(f32[2,16,1,768]{3,2,1,0:T(1,128)S(1)} %slice.16), channel_id=1, source_target_pairs={{0,2},{2,4},{4,6},{1,3},{3,5},{5,7},{8,10},{10,12},{12,14},{9,11},... | collective-permute-start | bytes 294920 | tf_op jit(solution)/shard_map/ppermute | solution.py:15
  35.5 16.6 %collective-permute-start.1 = (f32[2,16,1,768]{3,2,1,0:T(1,128)S(1)}, f32[2,16,1,768]{3,2,1,0:T(1,128)S(1)}, u32[]{:S(2)}, u32[]{:S(2)}) collective-permute-start(f32[2,16,1,768]{3,2,1,0:T(1,128)S(1)} %slice.18), channel_id=1, source_target_pairs={{0,2},{2,4},{4,6},{1,3},{3,5},{5,7},{8,10},{10,12},{12,14},{9,11},... | collective-permute-start | bytes 294920 | tf_op jit(solution)/shard_map/ppermute | solution.py:15
  79.3 208.1 %all-to-all-start = ((f32[2,16,96,768]{3,2,0,1:T(8,128)}), f32[2,16,96,768]{3,2,0,1:T(8,128)}, u32[]{:S(2)}, u32[]{:S(2)}) async-start(f32[2,16,96,768]{3,2,0,1:T(8,128)} %copy.11), calls=%async_computation | async-start | bytes 18874368 | tf_op jit(solution)/shard_map/all_to_all | solution.py:82
  287.4 108.9 %all-to-all-start.1 = ((bf16[2,16,96,768]{3,2,0,1:T(8,128)(2,1)}), bf16[2,16,96,768]{3,2,0,1:T(8,128)(2,1)}, u32[]{:S(2)}, u32[]{:S(2)}) async-start(bf16[2,16,96,768]{3,2,0,1:T(8,128)(2,1)} %copy.13), calls=%async_computation.1 | async-start | bytes 9437184 | tf_op jit(solution)/shard_map/all_to_all | solution.py:83
  300.4 3.7 copy-start.2
  304.2 4.7 copy-start.7
  306.8 96.9 %collective-permute-start.2 = (bf16[2,4,384,768]{3,2,1,0:T(8,128)(2,1)}, bf16[2,4,384,768]{3,2,1,0:T(8,128)(2,1)}, u32[]{:S(2)}, u32[]{:S(2)}) collective-permute-start(bf16[2,4,384,768]{3,2,1,0:T(8,128)(2,1)} %bitcast_convert_fusion), channel_id=1, source_target_pairs={{0,8},{8,16},{16,24},{1,9},{9,17},{17,25},{2,10},{10,18},{18,26},{... | collective-permute-start | bytes 14155784 | tf_op jit(solution)/shard_map/ppermute | solution.py:15
  396.4 15.7 %slice-start = ((s8[9437184]{0:T(1024)(128)(4,1)}), s8[4194304]{0:T(1024)(128)(4,1)S(1)}, s32[]{:S(2)}) async-start(s8[9437184]{0:T(1024)(128)(4,1)} %bitcast.80), calls=%async_computation.2 | async-start | bytes 8388608
  396.4 15.7 %slice-start.1 = ((s8[9437184]{0:T(1024)(128)(4,1)}), s8[4194304]{0:T(1024)(128)(4,1)S(1)}, s32[]{:S(2)}) async-start(s8[9437184]{0:T(1024)(128)(4,1)} %bitcast.80), calls=%async_computation.3 | async-start | bytes 8388608
  403.7 8.4 %slice-start.2 = ((s8[9437184]{0:T(1024)(128)(4,1)}), s8[1048576]{0:T(1024)(128)(4,1)S(1)}, s32[]{:S(2)}) async-start(s8[9437184]{0:T(1024)(128)(4,1)} %bitcast.80), calls=%async_computation.4 | async-start | bytes 2097152
  417.5 55.5 %collective-permute-start.3 = (bf16[2,4,384,768]{3,2,1,0:T(8,128)(2,1)S(1)}, bf16[2,4,384,768]{3,2,1,0:T(8,128)(2,1)}, u32[]{:S(2)}, u32[]{:S(2)}) collective-permute-start(bf16[2,4,384,768]{3,2,1,0:T(8,128)(2,1)S(1)} %fusion), channel_id=1, source_target_pairs={{0,8},{8,16},{16,24},{1,9},{9,17},{17,25},{2,10},{10,18},{18,26},{... | collective-permute-start | bytes 14155784 | tf_op jit(solution)/shard_map/ppermute | solution.py:15
  488.1 55.7 %collective-permute-start.4 = (bf16[2,4,384,768]{3,2,1,0:T(8,128)(2,1)}, bf16[2,4,384,768]{3,2,1,0:T(8,128)(2,1)}, u32[]{:S(2)}, u32[]{:S(2)}) collective-permute-start(bf16[2,4,384,768]{3,2,1,0:T(8,128)(2,1)} %fusion.1), channel_id=1, source_target_pairs={{0,8},{8,16},{16,24},{1,9},{9,17},{17,25},{2,10},{10,18},{18,26},{... | collective-permute-start | bytes 14155784 | tf_op jit(solution)/shard_map/ppermute | solution.py:15
  490.0 62.1 %slice-start.3 = ((s8[9437184]{0:T(1024)(128)(4,1)}), s8[1048576]{0:T(1024)(128)(4,1)S(1)}, s32[]{:S(2)}) async-start(s8[9437184]{0:T(1024)(128)(4,1)} %bitcast.82), calls=%async_computation.5 | async-start | bytes 2097152
  490.0 62.1 %slice-start.4 = ((s8[9437184]{0:T(1024)(128)(4,1)}), s8[4194304]{0:T(1024)(128)(4,1)S(1)}, s32[]{:S(2)}) async-start(s8[9437184]{0:T(1024)(128)(4,1)} %bitcast.82), calls=%async_computation.6 | async-start | bytes 8388608
  490.0 62.0 %slice-start.5 = ((s8[9437184]{0:T(1024)(128)(4,1)}), s8[4194304]{0:T(1024)(128)(4,1)S(1)}, s32[]{:S(2)}) async-start(s8[9437184]{0:T(1024)(128)(4,1)} %bitcast.82), calls=%async_computation.7 | async-start | bytes 8388608
  556.8 3.7 copy-start.4
  563.5 71.6 %collective-permute-start.5 = (f32[2,4,96,768]{3,2,1,0:T(8,128)}, f32[2,4,96,768]{3,2,1,0:T(8,128)}, u32[]{:S(2)}, u32[]{:S(2)}) collective-permute-start(f32[2,4,96,768]{3,2,1,0:T(8,128)} %get-tuple-element.7), channel_id=1, source_target_pairs={{0,2},{2,0},{4,6},{6,4},{1,3},{3,1},{5,7},{7,5},{8,10},{10,8},{12,... | collective-permute-start | bytes 7077896 | tf_op jit(solution)/shard_map/ppermute | solution.py:103
  566.9 131.8 %collective-permute-start.6 = (f32[2,4,96,768]{3,2,1,0:T(8,128)}, f32[2,4,96,768]{3,2,1,0:T(8,128)}, u32[]{:S(2)}, u32[]{:S(2)}) collective-permute-start(f32[2,4,96,768]{3,2,1,0:T(8,128)} %get-tuple-element.6), channel_id=1, source_target_pairs={{0,4},{2,6},{4,0},{6,2},{1,5},{3,7},{5,1},{7,3},{8,12},{10,14},{12... | collective-permute-start | bytes 7077896 | tf_op jit(solution)/shard_map/ppermute | solution.py:103
  566.9 158.9 %collective-permute-start.7 = (f32[2,4,96,768]{3,2,1,0:T(8,128)}, f32[2,4,96,768]{3,2,1,0:T(8,128)S(1)}, u32[]{:S(2)}, u32[]{:S(2)}) collective-permute-start(f32[2,4,96,768]{3,2,1,0:T(8,128)} %get-tuple-element.5), channel_id=1, source_target_pairs={{0,6},{2,4},{4,2},{6,0},{1,7},{3,5},{5,3},{7,1},{8,14},{10,12},{12... | collective-permute-start | bytes 7077896 | tf_op jit(solution)/shard_map/ppermute | solution.py:103
  568.4 159.1 %copy-start.1 = (bf16[768,768]{1,0:T(8,128)(2,1)S(1)}, bf16[768,768]{1,0:T(8,128)(2,1)}, u32[]{:S(2)}) copy-start(bf16[768,768]{1,0:T(8,128)(2,1)} %param.9) | copy-start | bytes 3538948
  700.6 25.2 %copy-start.6 = (f32[1,2,16,96,768]{4,3,2,1,0:T(8,128)}, f32[1,2,16,96,768]{4,3,2,1,0:T(8,128)S(1)}, u32[]{:S(2)}) copy-start(f32[1,2,16,96,768]{4,3,2,1,0:T(8,128)S(1)} %bitcast_dynamic-update-slice_fusion.1) | copy-start | bytes 28311556
